TPU v7x, 512 devices: a whole 4x4x16 slice. The times are simulated.
512 devices in a mesh: tensor: 64 (over x, z_lo, core), expert: 8 (over z_hi, y).
Axes of the slice: x: 4, y: 4, z: 16 (z_hi: 2, z_lo: 8; z = z_hi * 8 + z_lo), core: 2. Of those that a mesh axis runs over, the one named last changes fastest.
Arguments:
- acts: bfloat16 [384, 3072], P('expert', 'tensor'), may hold values from -6 to 6
- grad_out: bfloat16 [384, 3072], P('expert', 'tensor'), may hold values from -6 to 6
- routing: int32 [384, 2], P('expert'), may hold values from 0 to 7, all different within a row; in each aligned block of 48 rows (0 to 47, 48 to 95, ...) at most 24 rows name the same one
- gates: float32 [384, 2], P('expert'), may hold values from 0.1 to 1
- w_gate: bfloat16 [8, 3072, 8192], P('expert', None, 'tensor'), may hold values from -0.109375 to 0.109375
- w_up: bfloat16 [8, 3072, 8192], P('expert', None, 'tensor'), may hold values from -0.109375 to 0.109375
- w_down: bfloat16 [8, 8192, 3072], P('expert', 'tensor'), may hold values from -0.0625 to 0.0625
Outputs:
- grad_gate: bfloat16 [8, 3072, 8192], P('expert', None, 'tensor')
- grad_up: bfloat16 [8, 3072, 8192], P('expert', None, 'tensor')
- grad_down: bfloat16 [8, 8192, 3072], P('expert', 'tensor')
- grad_acts: bfloat16 [384, 3072], P('expert', 'tensor')
Inputs may be any that keep to these rules, and one draw needn't show every extreme that they name: `routing`: within the tokens of one owner group (aligned blocks of 48 rows) no expert is named more than 24 times, a bound that some block reaches; a token's two experts differ.
All inputs are finite; a program needn't handle non-finite values.
Results may differ from a plain program's by a relative error of at most 0.02.
Values may be sent and summed in bfloat16 or wider, within the bound.
A program may use at most 64 MiB of HBM per device.

v0:
```python
import jax
import jax.numpy as jnp
from jax import lax
from jax.sharding import PartitionSpec as P


def dispatch_table(routing, gates, experts, capacity):
    tok_count = routing.shape[0]
    entries = routing.reshape(-1)
    chosen = (entries[:, None] == jnp.arange(experts, dtype=jnp.int32)[None, :]).astype(jnp.int32)
    earlier = jnp.cumsum(chosen, axis=0) - chosen
    position = jnp.sum(earlier * chosen, axis=1)
    in_slot = (position[:, None] == jnp.arange(capacity, dtype=jnp.int32)[None, :]).astype(
        jnp.float32
    )
    placed = chosen.astype(jnp.float32)[:, :, None] * in_slot[:, None, :]
    placed = placed.reshape(tok_count, 2, experts, capacity)
    table = jnp.sum(placed, axis=1)
    gate_slot = jnp.einsum("tkec,tk->ec", placed, gates)
    return (table, gate_slot)


def contract_rows(left, right):
    return lax.dot_general(
        left, right, (((0,), (0,)), ((), ())), preferred_element_type=jnp.float32
    )


def contract_cols(left, right):
    return lax.dot_general(
        left, right, (((1,), (1,)), ((), ())), preferred_element_type=jnp.float32
    )


def body(acts, grad_out, routing, gates, w_gate, w_up, w_down):
    groups = lax.axis_size("expert")
    tok_count = routing.shape[0]
    capacity = min(tok_count, 4 * tok_count // groups)
    table, gate_slot = dispatch_table(routing, gates, groups, capacity)
    table_half = table.astype(jnp.bfloat16)

    def place_rows(source):
        return jnp.einsum("tec,td->ecd", table_half, source, preferred_element_type=jnp.float32)

    whole_acts, whole_grad = (
        lax.all_gather(acts, "tensor", axis=1, tiled=True),
        lax.all_gather(grad_out, "tensor", axis=1, tiled=True),
    )
    slot_acts = place_rows(whole_acts).astype(jnp.bfloat16)
    slot_grad = (place_rows(whole_grad) * gate_slot[:, :, None]).astype(jnp.bfloat16)
    rows_acts, rows_grad = (
        lax.all_to_all(slot_acts, "expert", split_axis=0, concat_axis=0, tiled=True),
        lax.all_to_all(slot_grad, "expert", split_axis=0, concat_axis=0, tiled=True),
    )
    width = rows_acts.shape[2]
    rows_acts = rows_acts.reshape(-1, width)
    rows_grad = rows_grad.reshape(-1, width)
    gate_shard = w_gate[0]
    up_shard = w_up[0]
    down_shard = w_down[0]
    gate_pre = jnp.dot(rows_acts, gate_shard, preferred_element_type=jnp.float32)
    up_pre = jnp.dot(rows_acts, up_shard, preferred_element_type=jnp.float32)
    gate_sig = jax.nn.sigmoid(gate_pre)
    gate_act = gate_pre * gate_sig
    hidden = (gate_act * up_pre).astype(jnp.bfloat16)
    grad_hidden = contract_cols(rows_grad, down_shard)
    grad_up_pre = (grad_hidden * gate_act).astype(jnp.bfloat16)
    grad_gate_pre = (grad_hidden * up_pre * gate_sig * (1.0 + gate_pre * (1.0 - gate_sig))).astype(
        jnp.bfloat16
    )
    grad_down = contract_rows(hidden, rows_grad).astype(jnp.bfloat16)
    grad_gate = contract_rows(rows_acts, grad_gate_pre).astype(jnp.bfloat16)
    grad_up = contract_rows(rows_acts, grad_up_pre).astype(jnp.bfloat16)
    partial_sum = lax.psum_scatter(
        contract_cols(gate_shard, grad_gate_pre) + contract_cols(up_shard, grad_up_pre),
        "tensor",
        scatter_dimension=0,
        tiled=True,
    )
    feature_count = partial_sum.shape[0]
    slot_back = partial_sum.astype(jnp.bfloat16).reshape(feature_count, groups, capacity)
    returned = lax.all_to_all(slot_back, "expert", split_axis=1, concat_axis=1, tiled=True)
    grad_acts = jnp.einsum(
        "tec,dec->td", table_half, returned, preferred_element_type=jnp.float32
    ).astype(jnp.bfloat16)
    return (grad_gate[None], grad_up[None], grad_down[None], grad_acts)


def solution(mesh):
    return jax.shard_map(
        body,
        mesh=mesh,
        in_specs=(
            P("expert", "tensor"),
            P("expert", "tensor"),
            P("expert", None),
            P("expert", None),
            P("expert", None, "tensor"),
            P("expert", None, "tensor"),
            P("expert", "tensor", None),
        ),
        out_specs=(
            P("expert", None, "tensor"),
            P("expert", None, "tensor"),
            P("expert", "tensor", None),
            P("expert", "tensor"),
        ),
        check_vma=False,
    )
```

profile of v0, /device:TPU:1, one launch (start us, length us, event | category | flops | bytes accessed | tf_op | source)
XLA Modules:
  0.0 829.4 jit_solution(6612203091331258242)
XLA Ops:
  7.2 0.0 copy-start
  7.2 0.8 convert_convert_fusion
  7.9 0.8 copy.21
  8.7 0.8 copy.23
  9.5 0.1 eq.47
  9.6 0.1 fusion.22
  9.7 0.1 reduce_window_sum.11
  9.8 0.2 select_reduce_fusion
  10.0 0.1 eq.51
  10.2 0.1 copy.22
  10.2 130.2 %all_gather.6 = bf16[48,3072]{0,1:T(8,128)(2,1)S(1)} all-gather(bf16[48,48]{0,1:T(8,128)(2,1)S(1)} %copy.23), channel_id=1, replica_groups=mesh['tensor'=64,'expert'=8] {'tensor'}, dimensions={1}, use_global_device_ids=true | all-gather | bytes 299520 | tf_op jit(solution)/shard_map/all_gather | solution.py:46
  140.4 1.5 convolution_convert_fusion
  141.9 0.0 copy-start.3
  141.9 0.0 copy-start.4
  141.9 14.0 %all-to-all-start = ((bf16[8,24,3072]{2,1,0:T(8,128)(2,1)}), bf16[8,24,3072]{2,1,0:T(8,128)(2,1)S(1)}, u32[]{:S(2)}, u32[]{:S(2)}) async-start(bf16[8,24,3072]{2,1,0:T(8,128)(2,1)} %convolution_convert_fusion), calls=%async_computation | async-start | bytes 2359296 | tf_op jit(solution)/shard_map/all_to_all | solution.py:52
  155.9 0.0 copy-done.3
  155.9 0.1 copy.25
  156.0 163.9 %all_gather.7 = bf16[48,3072]{0,1:T(8,128)(2,1)S(1)} all-gather(bf16[48,48]{0,1:T(8,128)(2,1)S(1)} %copy.25), channel_id=1, replica_groups=mesh['tensor'=64,'expert'=8] {'tensor'}, dimensions={1}, use_global_device_ids=true | all-gather | bytes 299520 | tf_op jit(solution)/shard_map/all_gather | solution.py:47
  319.9 0.0 copy-done.4
  319.9 0.2 fusion.17
  320.1 1.5 fusion.1
  321.6 0.0 all-to-all-done
  321.6 18.0 %all-to-all-start.1 = ((bf16[8,24,3072]{2,1,0:T(8,128)(2,1)}), bf16[8,24,3072]{2,1,0:T(8,128)(2,1)S(1)}, u32[]{:S(2)}, u32[]{:S(2)}) async-start(bf16[8,24,3072]{2,1,0:T(8,128)(2,1)} %fusion.1), calls=%async_computation.1 | async-start | bytes 2359296 | tf_op jit(solution)/shard_map/all_to_all | solution.py:53
  339.6 0.0 reduce-scatter.4.cloned.1.call-start
  339.7 0.0 copy-start.1
  339.7 0.0 copy-done
  339.7 0.5 fusion.8
  340.2 0.7 copy-done.1
  340.8 0.5 fusion.11
  341.3 21.7 %all-to-all-done.1 = bf16[8,24,3072]{2,1,0:T(8,128)(2,1)S(1)} async-done(((bf16[8,24,3072]{2,1,0:T(8,128)(2,1)}), bf16[8,24,3072]{2,1,0:T(8,128)(2,1)S(1)}, u32[]{:S(2)}, u32[]{:S(2)}) %all-to-all-start.1) | async-done | bytes 1179680 | tf_op jit(solution)/shard_map/all_to_all | solution.py:53
  363.0 1.6 multiply_convert_fusion.1
  364.6 0.0 copy-start.2
  364.6 0.5 fusion.6
  365.1 0.7 copy-done.2
  365.8 1.9 fusion
  367.7 3.4 copy.33
  371.1 0.0 reduce-scatter.4.cloned.1.call-update
  371.1 1.5 fusion.3
  372.6 1.3 fusion.4
  373.9 418.1 %reduce-scatter.4.cloned.1.call-done = f32[48,192]{1,0:T(8,128)} async-done(((f32[3072,192]{1,0:T(8,128)}), f32[48,192]{1,0:T(8,128)}) %reduce-scatter.4.cloned.1.call-update) | async-done | bytes 36880
  792.0 0.9 copy.34
  792.9 0.7 reshape.75
  793.6 14.2 %all-to-all-start.2 = ((bf16[8,2,576]{2,1,0:T(2,128)(2,1)}), bf16[8,2,576]{2,1,0:T(2,128)(2,1)S(1)}, u32[]{:S(2)}, u32[]{:S(2)}) async-start(bf16[8,2,576]{2,1,0:T(2,128)(2,1)} %reshape.75), calls=%async_computation.2 | async-start | bytes 40960 | tf_op jit(solution)/shard_map/all_to_all | solution.py:82
  807.8 1.5 fusion.2
  809.4 12.3 %all-to-all-done.2 = bf16[8,2,576]{2,1,0:T(2,128)(2,1)S(1)} async-done(((bf16[8,2,576]{2,1,0:T(2,128)(2,1)}), bf16[8,2,576]{2,1,0:T(2,128)(2,1)S(1)}, u32[]{:S(2)}, u32[]{:S(2)}) %all-to-all-start.2) | async-done | bytes 18464 | tf_op jit(solution)/shard_map/all_to_all | solution.py:82
  821.6 0.1 reshape.76
  821.8 0.8 fusion.5
  (2 shorter events, 0.0 us)
Async XLA Ops:
  7.2 332.5 %copy-start = (bf16[1,3072,128]{2,1,0:T(8,128)(2,1)S(1)}, bf16[1,3072,128]{2,1,0:T(8,128)(2,1)}, u32[]{:S(2)}) copy-start(bf16[1,3072,128]{2,1,0:T(8,128)(2,1)} %param.11) | copy-start | bytes 2359300
  141.9 14.0 %copy-start.3 = (bf16[48,48]{1,0:T(8,128)(2,1)S(1)}, bf16[48,48]{1,0:T(8,128)(2,1)}, u32[]{:S(2)}) copy-start(bf16[48,48]{1,0:T(8,128)(2,1)} %param.8) | copy-start | bytes 13828
  141.9 177.9 %copy-start.4 = (f32[48,2]{0,1:T(2,128)S(1)}, f32[48,2]{0,1:T(2,128)}, u32[]{:S(2)}) copy-start(f32[48,2]{0,1:T(2,128)} %param.10) | copy-start | bytes 1156
  141.9 179.7 %all-to-all-start = ((bf16[8,24,3072]{2,1,0:T(8,128)(2,1)}), bf16[8,24,3072]{2,1,0:T(8,128)(2,1)S(1)}, u32[]{:S(2)}, u32[]{:S(2)}) async-start(bf16[8,24,3072]{2,1,0:T(8,128)(2,1)} %convolution_convert_fusion), calls=%async_computation | async-start | bytes 2359296 | tf_op jit(solution)/shard_map/all_to_all | solution.py:52
  321.6 41.4 %all-to-all-start.1 = ((bf16[8,24,3072]{2,1,0:T(8,128)(2,1)}), bf16[8,24,3072]{2,1,0:T(8,128)(2,1)S(1)}, u32[]{:S(2)}, u32[]{:S(2)}) async-start(bf16[8,24,3072]{2,1,0:T(8,128)(2,1)} %fusion.1), calls=%async_computation.1 | async-start | bytes 2359296 | tf_op jit(solution)/shard_map/all_to_all | solution.py:53
  339.6 452.4 %reduce-scatter.4.cloned.1.call-start = ((), (), s32[]{:S(2)}) async-start(), calls=%async_computation.4 | async-start | bytes 3194880
  339.7 1.1 copy-start.1
  364.6 1.1 copy-start.2
  793.6 28.0 %all-to-all-start.2 = ((bf16[8,2,576]{2,1,0:T(2,128)(2,1)}), bf16[8,2,576]{2,1,0:T(2,128)(2,1)S(1)}, u32[]{:S(2)}, u32[]{:S(2)}) async-start(bf16[8,2,576]{2,1,0:T(2,128)(2,1)} %reshape.75), calls=%async_computation.2 | async-start | bytes 40960 | tf_op jit(solution)/shard_map/all_to_all | solution.py:82
Sparse Core Ops, SparseCore 0:
  371.2 420.7 reduce-scatter.3
where the time goes:
time: 833 us; the launch traced here: 829 us
  waiting for transfers between devices  452 us (54%)
  blocking collectives  294 us (35%)
  starting transfers between devices  46.2 us (6%)
  between operations  14.1 us (2%)
  matrix products  13.3 us (2%)
  local copies, waits for them, and re-layouts  8.43 us (1%)
    unnamed x2, waiting for transfers between devices  418 us
    all_gather x1, blocking collectives, body(): lax.all_gather(grad_out, 'tensor', axis=1, tiled=True)  164 us
    all_gather x1, blocking collectives, body(): lax.all_gather(acts, 'tensor', axis=1, tiled=True)  130 us
    all_to_all x1, waiting for transfers between devices, body(): lax.all_to_all(slot_grad, 'expert', split_axis=0, concat_axis=0, tiled=True)  21.7 us
    all_to_all x1, starting transfers between devices, body(): lax.all_to_all(slot_grad, 'expert', split_axis=0, concat_axis=0, tiled=True)  18 us
  transfers between devices with their start and end apart: 4, of which 3 were waited for; matrix products, arithmetic and copies ran while one was open for 1% of the time, Pallas kernels for 0%

commit v1 on v0

v1 whole, which is shorter than its diff:
```python
import jax
import jax.numpy as jnp
from jax import lax
from jax.experimental import pallas as pl
from jax.experimental.pallas import tpu as pltpu
from jax.sharding import PartitionSpec as P

NX, NZ, NC = 4, 8, 2
NH, NY = 2, 4
F = 48
T = 48
CAP = 24
E = NH * NY
ROWS = E * 2 * CAP
H = 128
K = NZ * NC * F
BF = jnp.bfloat16
F32 = jnp.float32
MESH = pl.DeviceIdType.MESH


def iota(shape, dim):
    return lax.broadcasted_iota(jnp.int32, shape, dim)


def split_rows(i):
    group = (i * 1366) >> 16
    rest = i - group * (2 * CAP)
    half = (rest >= CAP).astype(jnp.int32)
    return group, half, rest - half * CAP


def mm(a, b):
    return jnp.dot(a, b, preferred_element_type=F32)


def nt(a, b):
    return lax.dot_general(a, b, (((1,), (1,)), ((), ())), preferred_element_type=F32)


def kernel(
    acts, grad, routing, gates, wg, wu, wd,
    o_gate, o_up, o_down, o_acts,
    wgu, w3, send, recv, ag, acc, a01, hs, part, sib, xs, xr, zs, zr, back_s, back_r,
    s_w, s_a2a, r_a2a, r_ag, s_agz, s_agx, s_agc,
    s_sib, r_sib, s_x, r_x, s_z, r_z, s_back, r_back,
):
    tensor, expert = lax.axis_index("tensor"), lax.axis_index("expert")
    x, z, c = tensor // (NZ * NC), (tensor // NC) % NZ, tensor % NC
    zh, y = expert // NY, expert % NY

    def dev(x_, z_, c_, zh_, y_):
        return ((x_ * NZ + z_) * NC + c_, zh_ * NY + y_)

    def remote(src, dst, ss, rs, to):
        return pltpu.make_async_remote_copy(
            src_ref=src, dst_ref=dst, send_sem=ss, recv_sem=rs, device_id=to, device_id_type=MESH
        )

    sibling = dev(x, z, 1 - c, zh, y)

    barrier = pltpu.get_barrier_semaphore()

    def greet(to):
        pl.semaphore_signal(barrier, inc=1, device_id=to, device_id_type=MESH)

    for h in range(NH):
        for k in range(NY):
            if h or k:
                for cc in range(NC):
                    greet(dev(x, z, cc, (zh + h) % NH, (y + k) % NY))
    for k in range(1, NZ):
        greet(dev(x, (z + k) % NZ, c, zh, y))
    for k in range(1, NX):
        greet(dev((x + k) % NX, z, c, zh, y))
    greet(sibling)

    w_copies = [
        pltpu.make_async_copy(wg, wgu.at[:, :, :, :, pl.ds(0, H)], s_w.at[0]),
        pltpu.make_async_copy(wu, wgu.at[:, :, :, :, pl.ds(H, H)], s_w.at[1]),
    ] + [
        pltpu.make_async_copy(wd.at[:, pl.ds(q * K, K)], w3.at[q, pl.ds(2 * H, H), :], s_w.at[2 + q])
        for q in range(NX)
    ]
    for cp in w_copies:
        cp.start()

    r = routing[...]
    g = gates[...]
    r0, r1 = r[:, 0:1], r[:, 1:2]
    names = iota((T, E), 1)
    c0, c1 = (r0 == names).astype(F32), (r1 == names).astype(F32)
    before = (iota((T, T), 1) < iota((T, T), 0)).astype(BF)
    earlier = mm(before, (c0 + c1).astype(BF))
    pos0 = jnp.sum(earlier * c0, axis=1, keepdims=True)
    pos1 = jnp.sum((earlier + c0) * c1, axis=1, keepdims=True)
    key0 = jnp.where(pos0 < CAP, r0.astype(F32) * CAP + pos0, -1.0)
    key1 = jnp.where(pos1 < CAP, r1.astype(F32) * CAP + pos1, -1.0)
    eye = (iota((T, T), 0) == iota((T, T), 1)).astype(F32)

    def as_row(col):
        return jnp.sum(eye * col, axis=0, keepdims=True)

    group_c, half_c, slot_c = split_rows(iota((ROWS, 1), 0))
    want = (group_c * CAP + slot_c).astype(F32)
    m0 = (want == as_row(key0)).astype(F32)
    m1 = (want == as_row(key1)).astype(F32)
    gate_slot = jnp.sum(m0 * as_row(g[:, 0:1]) + m1 * as_row(g[:, 1:2]), axis=1, keepdims=True)
    onehot = (m0 + m1).astype(BF)
    rows = jnp.where(half_c == 0, mm(onehot, acts[...]), mm(onehot, grad[...]) * gate_slot)
    rows = jnp.concatenate([rows, jnp.zeros((ROWS, 128 - F), F32)], axis=1)
    send[...] = rows.astype(BF).reshape(E, 2 * CAP, 128)

    group_r, half_r, slot_r = split_rows(iota((1, ROWS), 1))
    want_r = (group_r * CAP + slot_r).astype(F32)
    mine = jnp.logical_and(jnp.logical_or(want_r == key0, want_r == key1), half_r == c)
    combine = mine.astype(BF)

    pl.semaphore_wait(barrier, 2 * (E - 1) + (NZ - 1) + (NX - 1) + 1)

    a2a = []
    for h in reversed(range(NH)):
        for k in range(NY):
            to_h, to_y = (zh + h) % NH, (y + k) % NY
            src, dst = send.at[to_h * NY + to_y], recv.at[h * NY + y]
            i = h * NY + k
            if h or k:
                from_y = (y + NY - k) % NY
                cp = remote(src, dst, s_a2a.at[i], r_a2a.at[i], dev(x, z, c, to_h, to_y))
            else:
                cp = pltpu.make_async_copy(src, dst, s_a2a.at[i])
            cp.start()
            a2a.append(cp)

    for cp in w_copies:
        cp.wait()
    for q in range(NX):
        w3[q, pl.ds(0, 2 * H), :] = wgu[q].reshape(K, 2 * H).T
    for cp in a2a:
        cp.wait()

    pick = (iota((F, 128), 0) == iota((F, 128), 1)).astype(BF)
    ag[x, z, c] = nt(pick, recv[...].reshape(ROWS, 128)).astype(BF)

    def ag_copy(bx, bz, ss, to):
        blk = ag.at[bx, bz, c]
        return remote(blk, blk, ss, r_ag.at[(bx * NZ + bz) * NC + c], to)

    def ag_arrived(bx, bz, bc):
        blk = ag.at[bx, bz, bc]
        remote(blk, blk, s_agz.at[0], r_ag.at[(bx * NZ + bz) * NC + bc], sibling).wait_recv()

    def z_send(k, _):
        ag_copy(x, z, s_agz.at[k], dev(x, (z + k) % NZ, c, zh, y)).start()
        return 0

    lax.fori_loop(1, NZ, z_send, 0)

    def x_send(bz):
        for k in (2, 1, 3):
            ag_copy(x, bz, s_agx.at[k * NZ + bz], dev((x + k) % NX, z, c, zh, y)).start()
        ag_copy(x, bz, s_agc.at[x * NZ + bz], sibling).start()

    x_send(z)

    def z_recv(k, _):
        bz = (z + k) % NZ
        ag_arrived(x, bz, c)
        x_send(bz)
        return 0

    lax.fori_loop(1, NZ, z_recv, 0)

    def block_dot(bx):
        return mm(w3[bx], ag[bx].reshape(K, ROWS))

    for k in (0, 1, 3, 2):
        bx = (x + k) % NX
        if k:
            def pass_on(i, _):
                ag_arrived(bx, (z + i) % NZ, c)
                ag_copy(bx, (z + i) % NZ, s_agc.at[bx * NZ + (z + i) % NZ], sibling).start()
                return 0

            lax.fori_loop(0, NZ, pass_on, 0)

        def other_core(i, _):
            ag_arrived(bx, i, 1 - c)
            return 0

        lax.fori_loop(0, NZ, other_core, 0)
        if k:
            acc[...] += block_dot(bx)
        else:
            acc[...] = block_dot(bx)

    _, lane_half, _ = split_rows(iota((H, ROWS), 1))
    is_x = lane_half == 0
    gate_pre, up_pre = acc[pl.ds(0, H), :], acc[pl.ds(H, H), :]
    grad_hidden = pltpu.roll(acc[pl.ds(2 * H, H), :], ROWS - CAP, 1)
    sig = 1.0 / (1.0 + jnp.exp(-gate_pre))
    act = gate_pre * sig
    zero = jnp.zeros((H, ROWS), F32)
    hidden = jnp.where(is_x, act * up_pre, zero)
    gup = jnp.where(is_x, grad_hidden * act, zero)
    ggp = jnp.where(is_x, grad_hidden * up_pre * sig * (1.0 + gate_pre * (1.0 - sig)), zero)
    gg = jnp.concatenate([ggp, gup], axis=0)
    a01[0] = gg.astype(BF)
    a01[1] = pltpu.roll(gg, CAP, 1).astype(BF)

    sib_copies, x_copies = {}, {}
    for k in (2, 1, 3, 0):
        bx = (x + k) % NX
        left0 = wgu[bx, :, 0].reshape(NZ * F, 2 * H)
        left1 = wgu[bx, :, 1].reshape(NZ * F, 2 * H)
        out = mm(left0, a01[0]) + mm(left1, a01[1])
        part[k] = out.astype(BF).reshape(NZ // NC, NC, F, ROWS)
        cp = remote(part.at[k, :, 1 - c], sib.at[k], s_sib.at[k], r_sib.at[k], sibling)
        cp.start()
        sib_copies[k] = cp
    for k in (2, 1, 3, 0):
        sib_copies[k].wait_recv()
        total = part[k, :, c].astype(F32) + sib[k].astype(F32)
        if k:
            xs[k] = total.astype(BF)
            cp = remote(xs.at[k], xr.at[k], s_x.at[k], r_x.at[k], dev((x + k) % NX, z, c, zh, y))
            cp.start()
            x_copies[k] = cp
        else:
            zs[...] = total

    hs[:, pl.ds(0, 2 * H)] = gg.T.astype(BF)
    hs[:, pl.ds(2 * H, H)] = pltpu.roll(hidden, CAP, 1).T.astype(BF)
    for q in range(NX):
        out = mm(ag[q].reshape(K, ROWS), hs[...])
        o_gate[pl.ds(q * K, K), :] = out[:, 0:H].astype(BF)
        o_up[pl.ds(q * K, K), :] = out[:, H : 2 * H].astype(BF)
        o_down[:, pl.ds(q * K, K)] = out[:, 2 * H :].T.astype(BF)

    for k in (1, 3, 2):
        x_copies[k].wait_recv()
        zs[...] += xr[k].astype(F32)
    half = zs[...].astype(BF)
    xs[0] = half

    def z_copy(q):
        return remote(
            xs.at[0, q], zr.at[z], s_z.at[q], r_z.at[z], dev(x, NC * q + c, c, zh, y)
        )

    for q in range(NZ // NC):
        @pl.when(NC * q + c != z)
        def _():
            z_copy(q).start()

    def back_place(h, k):
        return h * NY + k

    def back_copy(h, k, cc):
        to_h, to_y = (zh + h) % NH, (y + k) % NY
        return remote(
            back_s.at[h * NY + to_y], back_r.at[expert],
            s_back.at[(h * NY + k) * NC + cc], r_back.at[expert], dev(x, z, cc, to_h, to_y),
        )

    @pl.when(z % NC == c)
    def _():
        zr[z] = xs[0, z // NC]
        for k in range(1, NZ):
            bz = (z + k) % NZ
            remote(zr.at[bz], zr.at[bz], s_z.at[0], r_z.at[bz], sibling).wait_recv()
        total = jnp.sum(zr[...].astype(F32), axis=0).astype(BF)
        eye_f = (iota((ROWS, ROWS), 0) == iota((ROWS, ROWS), 1)).astype(BF)
        wide = jnp.concatenate([total, jnp.zeros((128 - F, ROWS), BF)], axis=0)
        rows = nt(eye_f, wide)
        back_s[...] = rows.astype(BF).reshape(E, 2 * CAP, 128)
        for h in reversed(range(NH)):
            for k in range(NY):
                if h or k:
                    for cc in range(NC):
                        back_copy(h, k, cc).start()
        remote(back_s.at[y], back_r.at[expert], s_back.at[0], r_back.at[expert], sibling).start()
        back_r[expert] = back_s[y]

    @pl.when(z % NC != c)
    def _():
        remote(back_s.at[y], back_r.at[expert], s_back.at[0], r_back.at[expert], sibling).wait_recv()

    for h in range(NH):
        for k in range(NY):
            if h or k:
                e2 = ((zh + h) % NH) * NY + (y + k) % NY
                remote(
                    back_s.at[0], back_r.at[e2], s_back.at[0], r_back.at[e2], sibling
                ).wait_recv()
    o_acts[...] = mm(combine, back_r[...].reshape(ROWS, 128))[:, 0:F].astype(BF)

    def z_sent(k, _):
        ag_copy(x, z, s_agz.at[k], sibling).wait_send()
        return 0

    lax.fori_loop(1, NZ, z_sent, 0)

    def x_sent(i, _):
        ag_copy(x, i % NZ, s_agx.at[i], sibling).wait_send()
        return 0

    lax.fori_loop(NZ, NX * NZ, x_sent, 0)

    def c_sent(i, _):
        ag_copy(x, z, s_agc.at[i], sibling).wait_send()
        return 0

    lax.fori_loop(0, NX * NZ, c_sent, 0)
    for cp in list(sib_copies.values()) + list(x_copies.values()):
        cp.wait_send()
    for q in range(NZ // NC):
        @pl.when(NC * q + c != z)
        def _():
            z_copy(q).wait_send()

    @pl.when(z % NC == c)
    def _():
        for h in range(NH):
            for k in range(NY):
                if h or k:
                    for cc in range(NC):
                        back_copy(h, k, cc).wait_send()
        remote(back_s.at[y], back_r.at[expert], s_back.at[0], r_back.at[expert], sibling).wait_send()


def body(acts, grad_out, routing, gates, w_gate, w_up, w_down):
    d = NX * K
    vm = pl.BlockSpec(memory_space=pltpu.VMEM)
    hbm = pl.BlockSpec(memory_space=pl.ANY)
    dma = pltpu.SemaphoreType.DMA
    out = pl.pallas_call(
        kernel,
        name="experts_backward",
        out_shape=(
            jax.ShapeDtypeStruct((d, H), BF),
            jax.ShapeDtypeStruct((d, H), BF),
            jax.ShapeDtypeStruct((H, d), BF),
            jax.ShapeDtypeStruct((T, F), BF),
        ),
        in_specs=[vm] * 4 + [hbm] * 3,
        out_specs=(vm,) * 4,
        scratch_shapes=[
            pltpu.VMEM((NX, NZ, NC, F, 2 * H), BF),
            pltpu.VMEM((NX, 3 * H, K), BF),
            pltpu.VMEM((E, 2 * CAP, 128), BF),
            pltpu.VMEM((E, 2 * CAP, 128), BF),
            pltpu.VMEM((NX, NZ, NC, F, ROWS), BF),
            pltpu.VMEM((3 * H, ROWS), F32),
            pltpu.VMEM((2, 2 * H, ROWS), BF),
            pltpu.VMEM((ROWS, 3 * H), BF),
            pltpu.VMEM((NX, NZ // NC, NC, F, ROWS), BF),
            pltpu.VMEM((NX, NZ // NC, F, ROWS), BF),
            pltpu.VMEM((NX, NZ // NC, F, ROWS), BF),
            pltpu.VMEM((NX, NZ // NC, F, ROWS), BF),
            pltpu.VMEM((NZ // NC, F, ROWS), F32),
            pltpu.VMEM((NZ, F, ROWS), BF),
            pltpu.VMEM((E, 2 * CAP, 128), BF),
            pltpu.VMEM((E, 2 * CAP, 128), BF),
            dma((2 + NX,)),
            dma((E,)),
            dma((E,)),
            dma((NX * NZ * NC,)),
            dma((NZ,)),
            dma((NX * NZ,)),
            dma((NX * NZ,)),
            dma((NX,)),
            dma((NX,)),
            dma((NX,)),
            dma((NX,)),
            dma((NZ // NC,)),
            dma((NZ,)),
            dma((E * NC,)),
            dma((E,)),
        ],
        compiler_params=pltpu.CompilerParams(
            collective_id=0, has_side_effects=True, vmem_limit_bytes=48 << 20
        ),
    )(
        acts,
        grad_out,
        routing,
        gates,
        w_gate.reshape(NX, NZ, NC, F, H),
        w_up.reshape(NX, NZ, NC, F, H),
        w_down.reshape(H, d),
    )
    return (out[0][None], out[1][None], out[2][None], out[3])


def solution(mesh):
    return jax.shard_map(
        body,
        mesh=mesh,
        in_specs=(
            P("expert", "tensor"),
            P("expert", "tensor"),
            P("expert", None),
            P("expert", None),
            P("expert", None, "tensor"),
            P("expert", None, "tensor"),
            P("expert", "tensor", None),
        ),
        out_specs=(
            P("expert", None, "tensor"),
            P("expert", None, "tensor"),
            P("expert", "tensor", None),
            P("expert", "tensor"),
        ),
        check_vma=False,
    )
```

time: 833 us -> 97.5 us (0.12)
  waiting for transfers between devices: 452 us -> 0 us
  blocking collectives: 294 us -> 0 us
  Pallas kernels: 0 us -> 87.8 us
  starting transfers between devices: 46.2 us -> 0 us
  between operations: 14.1 us -> 0.66 us
  matrix products: 13.3 us -> 0 us
    unnamed x2 -> x0, waiting for transfers between devices: 418 us -> none
    all_gather x2 -> x0, blocking collectives: 294 us -> none  [the longest x1 164 us: body(): lax.all_gather(grad_out, 'tensor', axis=1, tiled=True)]
    pallas_call x0 -> x1, Pallas kernels: none -> 87.8 us  [body(): pl.pallas_call(kernel, name='experts_backward', out_shape=(jax.ShapeDtype...]
    all_to_all x3 -> x0, starting transfers between devices: 46.2 us -> none  [the longest x1 18 us: body(): lax.all_to_all(slot_grad, 'expert', split_axis=0, concat_axis=0, tiled=True)]
    all_to_all x3 -> x0, waiting for transfers between devices: 34 us -> none  [the longest x1 21.7 us: body(): lax.all_to_all(slot_grad, 'expert', split_axis=0, concat_axis=0, tiled=True)]
    dot_general x12 -> x0, matrix products: 13.3 us -> none  [the longest x3 4.35 us: contract_rows(): lax.dot_general(left, right, (((0,), (0,)), ((), ())), preferred_element_...]
  transfers between devices with their start and end apart: 4 -> 0, of which waited for: 3 -> 0; matrix products, arithmetic and copies ran while one was open for 1% -> 0% of each run, Pallas kernels for 0% -> 0%
where the time goes in v1:
time: 97.5 us; the launch traced here: 97.1 us
  Pallas kernels  87.8 us (90%)
  local copies, waits for them, and re-layouts  8.71 us (9%)
    pallas_call x1, Pallas kernels, body(): pl.pallas_call(kernel, name='experts_backward', out_shape=(jax.ShapeDtype...  87.8 us
    unnamed x20, local copies, waits for them, and re-layouts  8.71 us

profile of v1, /device:TPU:1, one launch (start us, length us, event | category | flops | bytes accessed | tf_op | source)
XLA Modules:
  0.0 97.1 jit_solution(14910660821861573046)
XLA Ops:
  0.6 0.0 copy-start.5
  0.6 0.7 copy-done.5
  1.3 0.0 copy-start.6
  1.3 0.1 copy.11.routing
  1.4 0.6 copy-done.6
  2.0 0.0 copy-start.3
  2.0 0.0 copy-start.4
  2.0 0.1 copy.12.gates
  2.1 0.6 copy-done.3
  2.7 0.0 copy-done.4
  2.7 0.0 copy-start
  2.7 1.1 %copy-done = bf16[1,3072,128]{2,1,0:T(8,128)(2,1)S(1)} copy-done((bf16[1,3072,128]{2,1,0:T(8,128)(2,1)S(1)}, bf16[1,3072,128]{2,1,0:T(8,128)(2,1)}, u32[]{:S(2)}) %copy-start) | copy-done | bytes 786456
  3.8 0.0 copy-start.1
  3.9 1.1 %copy-done.1 = bf16[1,3072,128]{2,1,0:T(8,128)(2,1)S(1)} copy-done((bf16[1,3072,128]{2,1,0:T(8,128)(2,1)S(1)}, bf16[1,3072,128]{2,1,0:T(8,128)(2,1)}, u32[]{:S(2)}) %copy-start.1) | copy-done | bytes 786456
  5.0 0.0 copy-start.2
  5.0 1.1 %copy-done.2 = bf16[1,128,3072]{2,1,0:T(8,128)(2,1)S(1)} copy-done((bf16[1,128,3072]{2,1,0:T(8,128)(2,1)S(1)}, bf16[1,128,3072]{2,1,0:T(8,128)(2,1)}, u32[]{:S(2)}) %copy-start.2) | copy-done | bytes 786456
  6.1 87.8 %experts_backward.1 = (bf16[3072,128]{1,0:T(8,128)(2,1)S(1)}, bf16[3072,128]{1,0:T(8,128)(2,1)S(1)}, bf16[128,3072]{1,0:T(8,128)(2,1)S(1)}, bf16[48,48]{1,0:T(8,128)(2,1)S(1)}) custom-call(bf16[48,48]{1,0:T(8,128)(2,1)S(1)} %copy-done.3, bf16[48,48]{1,0:T(8,128)(2,1)S(1)} %copy-done.4, s32[48,2]{1,0:T(8,128)S(1)} %copy.11.routing, f32[48,2]{1,0:T(8,128)S(1)} %copy.12.gates, ...), custom_call_target="tpu_custom_call" | custom-call | tf_op jit(solution)/shard_map/experts_backward/pallas_call | solution.py:337
  93.9 0.9 copy.17
  94.8 0.9 copy.18
  95.6 0.9 copy.19
  96.5 0.6 copy.20
Async XLA Ops:
  0.6 0.7 copy-start.5
  1.3 0.7 copy-start.6
  2.0 0.7 copy-start.3
  2.0 0.7 copy-start.4
  2.7 1.1 %copy-start = (bf16[1,3072,128]{2,1,0:T(8,128)(2,1)S(1)}, bf16[1,3072,128]{2,1,0:T(8,128)(2,1)}, u32[]{:S(2)}) copy-start(bf16[1,3072,128]{2,1,0:T(8,128)(2,1)} %param.11) | copy-start | bytes 2359300
  3.8 1.1 %copy-start.1 = (bf16[1,3072,128]{2,1,0:T(8,128)(2,1)S(1)}, bf16[1,3072,128]{2,1,0:T(8,128)(2,1)}, u32[]{:S(2)}) copy-start(bf16[1,3072,128]{2,1,0:T(8,128)(2,1)} %param.12) | copy-start | bytes 2359300
  5.0 1.1 %copy-start.2 = (bf16[1,128,3072]{2,1,0:T(8,128)(2,1)S(1)}, bf16[1,128,3072]{2,1,0:T(8,128)(2,1)}, u32[]{:S(2)}) copy-start(bf16[1,128,3072]{2,1,0:T(8,128)(2,1)} %param.13) | copy-start | bytes 2359300

commit v2 on v1

v2 whole, which is shorter than its diff:
```python
import jax
import jax.numpy as jnp
from jax import lax
from jax.experimental import pallas as pl
from jax.experimental.pallas import tpu as pltpu
from jax.sharding import PartitionSpec as P

NX, NZ, NC = 4, 8, 2
NH, NY = 2, 4
F = 48
T = 48
CAP = 24
E = NH * NY
ROWS = E * 2 * CAP
MSG = E * CAP
NQ = NZ // NC
HALF = NZ // 2
W = 256
G0 = 64
ZF = NZ * F
H = 128
K = NZ * NC * F
BF = jnp.bfloat16
F32 = jnp.float32
MESH = pl.DeviceIdType.MESH


def iota(shape, dim):
    return lax.broadcasted_iota(jnp.int32, shape, dim)


def split(i, per):
    q = (i * (65536 // per + 1)) >> 16
    return q, i - q * per


def mm(a, b):
    return jnp.dot(a, b, preferred_element_type=F32)


def nt(a, b):
    return lax.dot_general(a, b, (((1,), (1,)), ((), ())), preferred_element_type=F32)


def swap_z(rows):
    half = rows.shape[0] // 2
    return jnp.concatenate([rows[half:], rows[:half]], axis=0)


def kernel(
    acts_h, grad_h, routing_h, gates_h, wg, wu, wd,
    o_gate, o_up, o_down, o_acts,
    acts, grad, routing, gates,
    wall, w3, send, recv, ag, acc, aw, hs, part, sib, xs, xr, zs, zr, back_s, back_r,
    s_in, s_w, s_a2a, r_a2a, r_ag, s_agz, s_agx, s_agf, s_agc,
    s_sib, r_sib, s_x, r_x, s_z, r_z, s_back, r_back,
):
    tensor, expert = lax.axis_index("tensor"), lax.axis_index("expert")
    x, z, c = tensor // (NZ * NC), (tensor // NC) % NZ, tensor % NC
    zh, y = expert // NY, expert % NY
    z4 = (z + HALF) % NZ

    def dev(x_, z_, c_, zh_, y_):
        return ((x_ * NZ + z_) * NC + c_, zh_ * NY + y_)

    def remote(src, dst, ss, rs, to):
        return pltpu.make_async_remote_copy(
            src_ref=src, dst_ref=dst, send_sem=ss, recv_sem=rs, device_id=to, device_id_type=MESH
        )

    sibling = dev(x, z, 1 - c, zh, y)

    barrier = pltpu.get_barrier_semaphore()

    def greet(to):
        pl.semaphore_signal(barrier, inc=1, device_id=to, device_id_type=MESH)

    for k in range(NY):
        for cc in range(NC):
            greet(dev(x, z4, cc, 1 - zh, (y + k) % NY))
    for k in range(1, NZ):
        greet(dev(x, (z + k) % NZ, c, zh, y))
    for k in range(1, NY):
        for cc in range(NC):
            greet(dev(x, z, cc, zh, (y + k) % NY))
    for k in range(1, NX):
        greet(dev((x + k) % NX, z, c, zh, y))
    greet(sibling)

    in_copies = [
        pltpu.make_async_copy(a, b, s_in.at[i])
        for i, (a, b) in enumerate(
            [(routing_h, routing), (gates_h, gates), (acts_h, acts), (grad_h, grad)]
        )
    ]
    w_copies = [
        pltpu.make_async_copy(wg, wall.at[:, :, :, :, pl.ds(0, H)], s_w.at[0]),
        pltpu.make_async_copy(wu, wall.at[:, :, :, :, pl.ds(H, H)], s_w.at[1]),
        pltpu.make_async_copy(wd, o_down, s_w.at[2]),
    ]
    for cp in in_copies + w_copies:
        cp.start()
    for cp in in_copies:
        cp.wait()

    r = routing[...]
    g = gates[...]
    r0, r1 = r[0:1, :], r[1:2, :]
    names = iota((E, T), 0)
    c0, c1 = (r0 == names).astype(F32), (r1 == names).astype(F32)
    before = (iota((T, T), 0) < iota((T, T), 1)).astype(BF)
    earlier = mm((c0 + c1).astype(BF), before)
    pos0 = jnp.sum(earlier * c0, axis=0, keepdims=True)
    pos1 = jnp.sum((earlier + c0) * c1, axis=0, keepdims=True)
    key0 = jnp.where(pos0 < CAP, r0.astype(F32) * CAP + pos0, -1.0)
    key1 = jnp.where(pos1 < CAP, r1.astype(F32) * CAP + pos1, -1.0)
    want = iota((MSG, 1), 0).astype(F32)
    m0 = (want == key0).astype(F32)
    m1 = (want == key1).astype(F32)
    gate_slot = jnp.sum(m0 * g[0:1, :] + m1 * g[1:2, :], axis=1, keepdims=True)
    onehot = (m0 + m1).astype(BF)
    gap = jnp.zeros((MSG, G0 - F), F32)
    rows = jnp.concatenate(
        [mm(onehot, acts[...]), gap, mm(onehot, grad[...]) * gate_slot, gap], axis=1
    )
    send[...] = rows.astype(BF).reshape(E, CAP, 128)

    pl.semaphore_wait(barrier, 2 * NY + (NZ - 1) + 2 * (NY - 1) + (NX - 1) + 1)

    here = c * NY + y

    def far_copy(k):
        to_y = (y + k) % NY
        return remote(
            send.at[(1 - zh) * NY + to_y], recv.at[here], s_a2a.at[NY + k], r_a2a.at[here],
            dev(x, z4, 1, 1 - zh, to_y),
        )

    def near_copy(k):
        to_y = (y + k) % NY
        return remote(
            send.at[zh * NY + to_y], recv.at[here], s_a2a.at[k], r_a2a.at[here],
            dev(x, z, 0, zh, to_y),
        )

    own_copy = pltpu.make_async_copy(send.at[expert], recv.at[here], s_a2a.at[0])
    for k in range(NY):
        far_copy(k).start()
    for k in (2, 1, 3):
        near_copy(k).start()

    @pl.when(c == 0)
    def _():
        own_copy.start()

    @pl.when(c == 1)
    def _():
        near_copy(0).start()

    for cp in w_copies:
        cp.wait()
    for q in range(NX):
        wall[q, :, :, :, pl.ds(2 * H, H)] = o_down[:, pl.ds(q * K, K)].T.reshape(NZ, NC, F, H)
        for cc in range(NC):
            w3[q, cc] = wall[q, :, cc].reshape(ZF, 3 * H).T
    g_r, rest_r = split(iota((MSG, ROWS), 1), 2 * CAP)
    row = iota((MSG, ROWS), 0)
    pick = iota((F, 128), 1) - iota((F, 128), 0)
    put_x = (row == g_r * CAP + rest_r).astype(BF) * (rest_r < CAP).astype(BF)
    put_g = (row == g_r * CAP + rest_r - CAP).astype(BF) * (rest_r >= CAP).astype(BF)
    pick_x, pick_g = (pick == 0).astype(BF), (pick == G0).astype(BF)

    @pl.when(c == 0)
    def _():
        own_copy.wait()

    def a2a_arrived(i, _):
        @pl.when(jnp.logical_or(c == 1, i != here))
        def _():
            remote(recv.at[i], recv.at[i], s_a2a.at[0], r_a2a.at[i], sibling).wait_recv()

        return 0

    lax.fori_loop(0, E, a2a_arrived, 0)
    got = recv[...].reshape(MSG, 128)
    x_t, g_t = nt(pick_x, got).astype(BF), nt(pick_g, got).astype(BF)
    ag[x, z, c] = (mm(x_t, put_x) + mm(g_t, put_g)).astype(BF)

    left, right, far = (x + NX - 1) % NX, (x + 1) % NX, (x + 2) % NX

    def near_z(j):
        return z // HALF * HALF + (z + j) % HALF

    def ag_copy(bx, bz, ss, to):
        blk = ag.at[bx, bz, c]
        return remote(blk, blk, ss, r_ag.at[(bx * NZ + bz) * NC + c], to)

    def ag_arrived(bx, bz, bc):
        blk = ag.at[bx, bz, bc]
        remote(blk, blk, s_agz.at[0], r_ag.at[(bx * NZ + bz) * NC + bc], sibling).wait_recv()

    def hub_copy():
        return ag_copy(x, z, s_agz.at[0], dev(x, z4, c, zh, y))

    def local_copies(bz):
        i = 1 + (bz // HALF + z // HALF) % 2 * (HALF - 1)
        return [
            ag_copy(x, bz, s_agz.at[i + j - 1], dev(x, near_z(j), c, zh, y))
            for j in range(1, HALF)
        ]

    def to_other_core(bx, bz):
        return ag_copy(bx, bz, s_agc.at[bx * NZ + bz], sibling)

    def x_copies_of(bz):
        return [
            ag_copy(x, bz, s_agx.at[bz], dev(right, z, c, zh, y)),
            ag_copy(x, bz, s_agx.at[NZ + bz], dev(left, z, c, zh, y)),
        ]

    def forward_right(bz):
        return ag_copy(left, bz, s_agf.at[bz], dev(right, z, c, zh, y))

    def forward_left(bz):
        return ag_copy(right, bz, s_agf.at[bz], dev(left, z, c, zh, y))

    def spread(bz):
        for cp in x_copies_of(bz):
            cp.start()
        to_other_core(x, bz).start()

    def z_arrived(bz):
        ag_arrived(x, bz, c)
        spread(bz)

    def x_arrived(bz):
        ag_arrived(left, bz, c)

        @pl.when(bz % 2 == 0)
        def _():
            forward_right(bz).start()

        to_other_core(left, bz).start()
        ag_arrived(right, bz, c)

        @pl.when(bz % 2 == 1)
        def _():
            forward_left(bz).start()

        to_other_core(right, bz).start()

    def far_arrived(bz):
        ag_arrived(far, bz, c)
        to_other_core(far, bz).start()

    def loop(n, f):
        def step(j, _):
            f(j)
            return 0

        lax.fori_loop(1, n, step, 0)

    def over(j):
        return (near_z(j) + HALF) % NZ

    hub_copy().start()
    for cp in x_copies_of(z):
        cp.start()
    for cp in local_copies(z):
        cp.start()
    to_other_core(x, z).start()
    loop(HALF, lambda j: z_arrived(near_z(j)))
    x_arrived(z)
    ag_arrived(x, z4, c)
    for cp in local_copies(z4):
        cp.start()
    spread(z4)
    loop(HALF, lambda j: x_arrived(near_z(j)))
    far_arrived(z)
    loop(HALF, lambda j: z_arrived(over(j)))
    x_arrived(z4)
    loop(HALF, lambda j: far_arrived(near_z(j)))
    loop(HALF, lambda j: x_arrived(over(j)))
    far_arrived(z4)
    loop(HALF, lambda j: far_arrived(over(j)))

    def block_of(bx, h):
        rows = ag[bx, :, h].reshape(ZF, ROWS)
        return swap_z(rows) if h else rows

    for k in (0, 1, 3, 2):
        bx = (x + k) % NX

        def other_core(i, _):
            ag_arrived(bx, i, 1 - c)
            return 0

        lax.fori_loop(0, NZ, other_core, 0)
        for h in range(NH):
            rows = block_of(bx, h)
            for cc in range(NC):
                new = mm(w3[bx, cc], rows[:, cc * 128 : cc * 128 + W])
                if k:
                    acc[h, cc] += new
                else:
                    acc[h, cc] = new

    both = [acc[h, 0] + pltpu.roll(acc[h, 1], W - G0, 1) for h in range(NH)]
    pre = jnp.concatenate(both, axis=1)
    lane = iota((H, NH * W), 1) & (W - 1)
    is_x = jnp.logical_and(split(lane, 2 * CAP)[1] < CAP, lane < ROWS // 2)
    gate_pre, up_pre = pre[0:H], pre[H : 2 * H]
    grad_hidden = pltpu.roll(pre[2 * H :], NH * W - CAP, 1)
    sig = 1.0 / (1.0 + jnp.exp(-gate_pre))
    act = gate_pre * sig
    zero = jnp.zeros((H, NH * W), F32)
    hidden = jnp.where(is_x, act * up_pre, zero)
    gup = jnp.where(is_x, grad_hidden * act, zero)
    ggp = jnp.where(is_x, grad_hidden * up_pre * sig * (1.0 + gate_pre * (1.0 - sig)), zero)
    gg = jnp.concatenate([ggp, gup], axis=0)
    for h in range(NH):
        own = gg[:, h * W : (h + 1) * W]
        for cc in range(NC):
            shift = h * G0 + cc * CAP
            aw[h, pl.ds(cc * 2 * H, 2 * H), :] = (
                pltpu.roll(own, shift, 1) if shift else own
            ).astype(BF)

    sib_copies = {}
    for k in (2, 1, 3, 0):
        bx = (x + k) % NX
        lhs = jnp.concatenate(
            [wall[bx, :, cc, :, pl.ds(0, 2 * H)].reshape(ZF, 2 * H) for cc in range(NC)], axis=1
        )
        p0, p1 = mm(lhs, aw[0]), swap_z(mm(lhs, aw[1]))
        out = jnp.concatenate([p0[:, 0:128], p0[:, 128:] + p1[:, 0:128], p1[:, 128:]], axis=1)
        part[k] = out.astype(BF).reshape(NQ, NC, F, ROWS)
        cp = remote(part.at[k, :, 1 - c], sib.at[k], s_sib.at[k], r_sib.at[k], sibling)
        cp.start()
        sib_copies[k] = cp

    def turn(i):
        return (z // NC + NQ // 2 + i) % NQ

    def x_copy(k, q):
        return remote(
            xs.at[k, q], xr.at[k, q], s_x.at[k * NQ + q], r_x.at[k * NQ + q],
            dev((x + k) % NX, z, c, zh, y),
        )

    for k in (2, 1, 3, 0):
        sib_copies[k].wait_recv()
        total = part[k, :, c].astype(F32) + sib[k].astype(F32)
        if k:
            xs[k] = total.astype(BF)
        else:
            zs[...] = total
        if k == 2:
            for i in range(NQ):
                x_copy(k, turn(i)).start()
        if k == 3:
            for i in range(NQ):
                x_copy(1, turn(i)).start()
                x_copy(3, turn(i)).start()

    for h in range(NH):
        cols = slice(h * W, (h + 1) * W)
        own = jnp.concatenate([gg[:, cols], pltpu.roll(hidden[:, cols], CAP, 1)], axis=0)
        for cc in range(NC):
            hs[h, cc] = (pltpu.roll(own, G0, 1) if cc else own).T.astype(BF)

    def weight_grads(q):
        downs = []
        rows = [block_of(q, h) for h in range(NH)]
        for cc in range(NC):
            cols = slice(cc * 128, cc * 128 + W)
            out = mm(rows[0][:, cols], hs[0, cc]) + mm(rows[1][:, cols], hs[1, cc])
            out = out.astype(BF).reshape(NZ, F, 3 * H)
            o_gate[q, :, cc] = out[:, :, 0:H]
            o_up[q, :, cc] = out[:, :, H : 2 * H]
            downs.append(out[:, :, 2 * H :])
        o_down[:, pl.ds(q * K, K)] = jnp.stack(downs, axis=1).reshape(K, H).T

    def z_copy(q):
        return remote(xs.at[0, q], zr.at[z], s_z.at[q], r_z.at[z], dev(x, NC * q + c, c, zh, y))

    for i in range(NQ):
        weight_grads(i)
        q = turn(i)
        for k in (2, 1, 3):
            x_copy(k, q).wait_recv()
        total = zs[q] + xr[1, q].astype(F32) + xr[2, q].astype(F32) + xr[3, q].astype(F32)
        xs[0, q] = total.astype(BF)

        @pl.when(NC * q + c != z)
        def _():
            z_copy(q).start()

    def back_copy(h, k, cc):
        to_y = (y + k) % NY
        i = (h * NY + k) * NC + cc
        to = dev(x, z4, cc, 1 - zh, to_y) if h else dev(x, z, cc, zh, to_y)
        return remote(
            back_s.at[(h * NY + to_y) * NC + cc], back_r.at[expert],
            s_back.at[i], r_back.at[expert], to,
        )

    own_back = remote(
        back_s.at[y * NC + 1 - c], back_r.at[expert], s_back.at[0], r_back.at[expert], sibling
    )
    back_list = [(h, k, cc) for h in (1, 0) for k in range(NY) for cc in range(NC) if h or k]

    @pl.when(z % NC == c)
    def _():
        zr[z] = xs[0, z // NC]
        for k in range(1, NZ):
            bz = (z + k) % NZ
            remote(zr.at[bz], zr.at[bz], s_z.at[0], r_z.at[bz], sibling).wait_recv()
        total = jnp.sum(zr[...].astype(F32), axis=0).astype(BF)
        eye_f = (iota((ROWS, ROWS), 0) == iota((ROWS, ROWS), 1)).astype(BF)
        wide = jnp.concatenate([total, jnp.zeros((128 - F, ROWS), BF)], axis=0)
        back_s[...] = nt(eye_f, wide).astype(BF).reshape(E * NC, CAP, 128)
        for args in back_list:
            back_copy(*args).start()
        own_back.start()
        back_r[expert] = back_s[y * NC + c]

    eye = (iota((T, T), 0) == iota((T, T), 1)).astype(F32)

    def as_col(row):
        return jnp.sum(eye * row, axis=1, keepdims=True)

    want_r = iota((1, MSG), 1).astype(F32)
    combine = jnp.logical_or(want_r == as_col(key0), want_r == as_col(key1)).astype(BF)

    def back_arrived(i, _):
        @pl.when(jnp.logical_or(z % NC != c, i != expert))
        def _():
            remote(back_r.at[i], back_r.at[i], s_back.at[0], r_back.at[i], sibling).wait_recv()

        return 0

    lax.fori_loop(0, E, back_arrived, 0)
    o_acts[...] = mm(combine, back_r[...].reshape(MSG, 128))[:, 0:F].astype(BF)

    for k in range(NY):
        far_copy(k).wait_send()
    for k in range(1, NY):
        near_copy(k).wait_send()

    @pl.when(c == 1)
    def _():
        near_copy(0).wait_send()

    hub_copy().wait_send()
    for cp in local_copies(z) + local_copies(z4):
        cp.wait_send()

    def x_sent(i, _):
        for cp in x_copies_of(i):
            cp.wait_send()
        forward_right(i).wait_send()
        return 0

    lax.fori_loop(0, NZ, x_sent, 0)

    def c_sent(i, _):
        to_other_core(i // NZ, i % NZ).wait_send()
        return 0

    lax.fori_loop(0, NX * NZ, c_sent, 0)
    for cp in sib_copies.values():
        cp.wait_send()
    for k in range(1, NX):
        for q in range(NQ):
            x_copy(k, q).wait_send()
    for q in range(NQ):
        @pl.when(NC * q + c != z)
        def _():
            z_copy(q).wait_send()

    @pl.when(z % NC == c)
    def _():
        for args in back_list:
            back_copy(*args).wait_send()
        own_back.wait_send()


def put(*refs):
    n = len(refs) // 2
    sems = refs[-1]
    copies = [pltpu.make_async_copy(refs[i], refs[n + i], sems.at[i]) for i in range(n)]
    for cp in copies:
        cp.start()
    for cp in copies:
        cp.wait()


def body(acts, grad_out, routing, gates, w_gate, w_up, w_down):
    d = NX * K
    vm = pl.BlockSpec(memory_space=pltpu.VMEM)
    hbm = pl.BlockSpec(memory_space=pltpu.HBM)
    dma = pltpu.SemaphoreType.DMA
    shapes = (
        jax.ShapeDtypeStruct((NX, NZ, NC, F, H), BF),
        jax.ShapeDtypeStruct((NX, NZ, NC, F, H), BF),
        jax.ShapeDtypeStruct((H, d), BF),
        jax.ShapeDtypeStruct((T, F), BF),
    )
    out = pl.pallas_call(
        kernel,
        name="experts_backward",
        out_shape=shapes,
        in_specs=[hbm] * 7,
        out_specs=(vm,) * 4,
        scratch_shapes=[
            pltpu.VMEM((T, F), BF),
            pltpu.VMEM((T, F), BF),
            pltpu.VMEM((2, T), jnp.int32),
            pltpu.VMEM((2, T), F32),
            pltpu.VMEM((NX, NZ, NC, F, 3 * H), BF),
            pltpu.VMEM((NX, NC, 3 * H, ZF), BF),
            pltpu.VMEM((E, CAP, 128), BF),
            pltpu.VMEM((E, CAP, 128), BF),
            pltpu.VMEM((NX, NZ, NC, F, ROWS), BF),
            pltpu.VMEM((NH, NC, 3 * H, W), F32),
            pltpu.VMEM((NH, NC * 2 * H, W), BF),
            pltpu.VMEM((NH, NC, W, 3 * H), BF),
            pltpu.VMEM((NX, NQ, NC, F, ROWS), BF),
            pltpu.VMEM((NX, NQ, F, ROWS), BF),
            pltpu.VMEM((NX, NQ, F, ROWS), BF),
            pltpu.VMEM((NX, NQ, F, ROWS), BF),
            pltpu.VMEM((NQ, F, ROWS), F32),
            pltpu.VMEM((NZ, F, ROWS), BF),
            pltpu.VMEM((E * NC, CAP, 128), BF),
            pltpu.VMEM((E, CAP, 128), BF),
            dma((4,)),
            dma((3,)),
            dma((E,)),
            dma((E,)),
            dma((NX * NZ * NC,)),
            dma((2 * HALF - 1,)),
            dma((2 * NZ,)),
            dma((NZ,)),
            dma((NX * NZ,)),
            dma((NX,)),
            dma((NX,)),
            dma((NX * NQ,)),
            dma((NX * NQ,)),
            dma((NQ,)),
            dma((NZ,)),
            dma((E * NC,)),
            dma((E,)),
        ],
        compiler_params=pltpu.CompilerParams(
            collective_id=0, has_side_effects=True, vmem_limit_bytes=40 << 20
        ),
    )(
        *[
            pltpu.with_memory_space_constraint(a, pltpu.HBM)
            for a in (
                acts,
                grad_out,
                routing.T,
                gates.T,
                w_gate.reshape(NX, NZ, NC, F, H),
                w_up.reshape(NX, NZ, NC, F, H),
                w_down.reshape(H, d),
            )
        ]
    )
    shapes = (jax.ShapeDtypeStruct((d, H), BF),) * 2 + shapes[2:]
    out = pl.pallas_call(
        put,
        name="put",
        out_shape=shapes,
        in_specs=[pl.BlockSpec(memory_space=pl.ANY)] * 4,
        out_specs=(hbm,) * 4,
        scratch_shapes=[dma((4,))],
        compiler_params=pltpu.CompilerParams(vmem_limit_bytes=1 << 20),
    )(out[0].reshape(d, H), out[1].reshape(d, H), out[2], out[3])
    return (out[0][None], out[1][None], out[2][None], out[3])


def solution(mesh):
    return jax.shard_map(
        body,
        mesh=mesh,
        in_specs=(
            P("expert", "tensor"),
            P("expert", "tensor"),
            P("expert", None),
            P("expert", None),
            P("expert", None, "tensor"),
            P("expert", None, "tensor"),
            P("expert", "tensor", None),
        ),
        out_specs=(
            P("expert", None, "tensor"),
            P("expert", None, "tensor"),
            P("expert", "tensor", None),
            P("expert", "tensor"),
        ),
        check_vma=False,
    )
```

time: 97.5 us -> 70.4 us (0.72)
  Pallas kernels: 87.8 us -> 69.6 us
  local copies, waits for them, and re-layouts: 8.71 us -> 0 us
    pallas_call x1 -> x2, Pallas kernels: 87.8 us -> 69.6 us  [the longest x1 68.2 us: body(): pl.pallas_call(kernel, name='experts_backward', out_shape=shapes, in_spec...]
    unnamed x20 -> x0, local copies, waits for them, and re-layouts: 8.71 us -> none
where the time goes in v2:
time: 70.4 us; the launch traced here: 70.3 us
  Pallas kernels  69.6 us (99%)
    pallas_call x1, Pallas kernels, body(): pl.pallas_call(kernel, name='experts_backward', out_shape=shapes, in_spec...  68.2 us
    pallas_call x1, Pallas kernels, body(): pl.pallas_call(put, name='put', out_shape=shapes, in_specs=[pl.BlockSpec(...  1.44 us

profile of v2, /device:TPU:1, one launch (start us, length us, event | category | flops | bytes accessed | tf_op | source)
XLA Modules:
  0.0 70.3 jit_solution(7864067125083063825)
XLA Ops:
  0.6 68.2 %experts_backward.1 = (bf16[4,8,2,48,128]{4,3,2,1,0:T(8,128)(2,1)S(1)}, bf16[4,8,2,48,128]{4,3,2,1,0:T(8,128)(2,1)S(1)}, bf16[128,3072]{1,0:T(8,128)(2,1)S(1)}, bf16[48,48]{1,0:T(8,128)(2,1)S(1)}) custom-call(bf16[48,48]{1,0:T(8,128)(2,1)} %acts_h.1, bf16[48,48]{1,0:T(8,128)(2,1)} %grad_h.1, s32[2,48]{1,0:T(2,128)} %bitcast.15, f32[2,48]{1,0:T(2,128)} %bitcast.16, ...), custom_call_target="tpu_custom_call" | custom-call | tf_op jit(solution)/shard_map/experts_backward/pallas_call | solution.py:510
  68.8 1.4 %put.1 = (bf16[3072,128]{1,0:T(8,128)(2,1)}, bf16[3072,128]{1,0:T(8,128)(2,1)}, bf16[128,3072]{1,0:T(8,128)(2,1)}, bf16[48,48]{1,0:T(8,128)(2,1)}) custom-call(bf16[3072,128]{1,0:T(8,128)(2,1)S(1)} %bitcast.10, bf16[3072,128]{1,0:T(8,128)(2,1)S(1)} %bitcast.11, bf16[128,3072]{1,0:T(8,128)(2,1)S(1)} %get-tuple-element.14.refs_2_, ...), custom_call_target="tpu_custom_call" | custom-call | tf_op jit(solution)/shard_map/put/pallas_call | solution.py:573

commit v3 on v2

--- a/solution.py
+++ b/solution.py
@@ -18,6 +18,7 @@
 W = 256
 G0 = 64
 ZF = NZ * F
+PARTS = ((128, 256), (0, 128))
 H = 128
 K = NZ * NC * F
 BF = jnp.bfloat16
@@ -127,6 +128,12 @@
 
     pl.semaphore_wait(barrier, 2 * NY + (NZ - 1) + 2 * (NY - 1) + (NX - 1) + 1)
 
+    unsent = []
+
+    def finish():
+        for f in unsent:
+            f()
+
     here = c * NY + y
 
     def far_copy(k):
@@ -156,6 +163,18 @@
     @pl.when(c == 1)
     def _():
         near_copy(0).start()
+
+    def a2a_sent():
+        for k in range(NY):
+            far_copy(k).wait_send()
+        for k in range(1, NY):
+            near_copy(k).wait_send()
+
+        @pl.when(c == 1)
+        def _():
+            near_copy(0).wait_send()
+
+    unsent.append(a2a_sent)
 
     for cp in w_copies:
         cp.wait()
@@ -224,7 +243,14 @@
     def forward_left(bz):
         return ag_copy(right, bz, s_agf.at[bz], dev(left, z, c, zh, y))
 
+    def unicast(bz):
+        return bz // HALF != z // HALF
+
     def spread(bz):
+        @pl.when(unicast(bz))
+        def _():
+            ag_copy(x, bz, s_agf.at[bz], dev(far, z, c, zh, y)).start()
+
         for cp in x_copies_of(bz):
             cp.start()
         to_other_core(x, bz).start()
@@ -236,14 +262,14 @@
     def x_arrived(bz):
         ag_arrived(left, bz, c)
 
-        @pl.when(bz % 2 == 0)
+        @pl.when(jnp.logical_and(bz % 2 == 0, jnp.logical_not(unicast(bz))))
         def _():
             forward_right(bz).start()
 
         to_other_core(left, bz).start()
         ag_arrived(right, bz, c)
 
-        @pl.when(bz % 2 == 1)
+        @pl.when(jnp.logical_and(bz % 2 == 1, jnp.logical_not(unicast(bz))))
         def _():
             forward_left(bz).start()
 
@@ -284,6 +310,26 @@
     far_arrived(z4)
     loop(HALF, lambda j: far_arrived(over(j)))
 
+    def gather_sent():
+        hub_copy().wait_send()
+        for cp in local_copies(z) + local_copies(z4):
+            cp.wait_send()
+
+        def x_sent(i, _):
+            for cp in x_copies_of(i):
+                cp.wait_send()
+            forward_right(i).wait_send()
+            return 0
+
+        lax.fori_loop(0, NZ, x_sent, 0)
+
+        def c_sent(i, _):
+            to_other_core(i // NZ, i % NZ).wait_send()
+            return 0
+
+        lax.fori_loop(0, NX * NZ, c_sent, 0)
+
+    unsent.append(gather_sent)
     def block_of(bx, h):
         rows = ag[bx, :, h].reshape(ZF, ROWS)
         return swap_z(rows) if h else rows
@@ -339,12 +385,20 @@
         cp.start()
         sib_copies[k] = cp
 
+    unsent.append(lambda: [cp.wait_send() for cp in sib_copies.values()])
     def turn(i):
-        return (z // NC + NQ // 2 + i) % NQ
-
-    def x_copy(k, q):
+        pair, lower = z // NC, 1 - z // HALF
+        if i < NQ // 2:
+            return lower * (NQ - 1 - i) + (1 - lower) * i
+        return pair if i == NQ - 1 else lower * (1 - pair) + (1 - lower) * (NQ + 1 - pair)
+
+    def cols(p):
+        return pl.ds(*PARTS[p])
+
+    def x_copy(k, q, p):
+        i = (p * NX + k) * NQ + q
         return remote(
-            xs.at[k, q], xr.at[k, q], s_x.at[k * NQ + q], r_x.at[k * NQ + q],
+            xs.at[k, q, :, cols(p)], xr.at[k, q, :, cols(p)], s_x.at[i], r_x.at[i],
             dev((x + k) % NX, z, c, zh, y),
         )
 
@@ -353,19 +407,26 @@
         total = part[k, :, c].astype(F32) + sib[k].astype(F32)
         if k:
             xs[k] = total.astype(BF)
+            x_copy(k, turn(0), 0).start()
         else:
             zs[...] = total
-        if k == 2:
-            for i in range(NQ):
-                x_copy(k, turn(i)).start()
         if k == 3:
-            for i in range(NQ):
-                x_copy(1, turn(i)).start()
-                x_copy(3, turn(i)).start()
+            for p in range(2):
+                for i in range(1 - p, NQ):
+                    for kk in (2, 1, 3):
+                        x_copy(kk, turn(i), p).start()
+
+    def x_left():
+        for k in range(1, NX):
+            for q in range(NQ):
+                for p in range(2):
+                    x_copy(k, q, p).wait_send()
+
+    unsent.append(x_left)
 
     for h in range(NH):
-        cols = slice(h * W, (h + 1) * W)
-        own = jnp.concatenate([gg[:, cols], pltpu.roll(hidden[:, cols], CAP, 1)], axis=0)
+        cut = slice(h * W, (h + 1) * W)
+        own = jnp.concatenate([gg[:, cut], pltpu.roll(hidden[:, cut], CAP, 1)], axis=0)
         for cc in range(NC):
             hs[h, cc] = (pltpu.roll(own, G0, 1) if cc else own).T.astype(BF)
 
@@ -373,29 +434,44 @@
         downs = []
         rows = [block_of(q, h) for h in range(NH)]
         for cc in range(NC):
-            cols = slice(cc * 128, cc * 128 + W)
-            out = mm(rows[0][:, cols], hs[0, cc]) + mm(rows[1][:, cols], hs[1, cc])
+            cut = slice(cc * 128, cc * 128 + W)
+            out = mm(rows[0][:, cut], hs[0, cc]) + mm(rows[1][:, cut], hs[1, cc])
             out = out.astype(BF).reshape(NZ, F, 3 * H)
             o_gate[q, :, cc] = out[:, :, 0:H]
             o_up[q, :, cc] = out[:, :, H : 2 * H]
             downs.append(out[:, :, 2 * H :])
         o_down[:, pl.ds(q * K, K)] = jnp.stack(downs, axis=1).reshape(K, H).T
 
-    def z_copy(q):
-        return remote(xs.at[0, q], zr.at[z], s_z.at[q], r_z.at[z], dev(x, NC * q + c, c, zh, y))
-
-    for i in range(NQ):
-        weight_grads(i)
-        q = turn(i)
-        for k in (2, 1, 3):
-            x_copy(k, q).wait_recv()
-        total = zs[q] + xr[1, q].astype(F32) + xr[2, q].astype(F32) + xr[3, q].astype(F32)
-        xs[0, q] = total.astype(BF)
-
-        @pl.when(NC * q + c != z)
-        def _():
-            z_copy(q).start()
-
+    def z_copy(q, p):
+        return remote(
+            xs.at[0, q, :, cols(p)], zr.at[z, :, cols(p)], s_z.at[p * NQ + q],
+            r_z.at[p * NZ + z], dev(x, NC * q + c, c, zh, y),
+        )
+
+    for p in range(2):
+        for i in range(NQ):
+            if p == 0:
+                weight_grads(i)
+            q = turn(i)
+            for k in (2, 1, 3):
+                x_copy(k, q, p).wait_recv()
+            total = zs[q, :, cols(p)]
+            for k in (1, 2, 3):
+                total += xr[k, q, :, cols(p)].astype(F32)
+            xs[0, q, :, cols(p)] = total.astype(BF)
+
+            @pl.when(NC * q + c != z)
+            def _():
+                z_copy(q, p).start()
+
+    def z_sent():
+        for q in range(NQ):
+            @pl.when(NC * q + c != z)
+            def _():
+                for p in range(2):
+                    z_copy(q, p).wait_send()
+
+    unsent.append(z_sent)
     def back_copy(h, k, cc):
         to_y = (y + k) % NY
         i = (h * NY + k) * NC + cc
@@ -412,18 +488,32 @@
 
     @pl.when(z % NC == c)
     def _():
-        zr[z] = xs[0, z // NC]
-        for k in range(1, NZ):
-            bz = (z + k) % NZ
-            remote(zr.at[bz], zr.at[bz], s_z.at[0], r_z.at[bz], sibling).wait_recv()
-        total = jnp.sum(zr[...].astype(F32), axis=0).astype(BF)
-        eye_f = (iota((ROWS, ROWS), 0) == iota((ROWS, ROWS), 1)).astype(BF)
-        wide = jnp.concatenate([total, jnp.zeros((128 - F, ROWS), BF)], axis=0)
-        back_s[...] = nt(eye_f, wide).astype(BF).reshape(E * NC, CAP, 128)
-        for args in back_list:
-            back_copy(*args).start()
+        eye_f = (iota((W, W), 0) == iota((W, W), 1)).astype(BF)
+        for p in range(2):
+            zr[z, :, cols(p)] = xs[0, z // NC, :, cols(p)]
+            for k in range(1, NZ):
+                bz = (z + k) % NZ
+                blk = zr.at[bz, :, cols(p)]
+                remote(blk, blk, s_z.at[0], r_z.at[p * NZ + bz], sibling).wait_recv()
+            h = 1 - p
+            total = jnp.sum(zr[:, :, h * 128 : h * 128 + W].astype(F32), axis=0).astype(BF)
+            wide = jnp.concatenate([total, jnp.zeros((128 - F, W), BF)], axis=0)
+            rows = nt(eye_f, wide)[h * G0 : h * G0 + MSG]
+            back_s[h * E : (h + 1) * E] = rows.astype(BF).reshape(E, CAP, 128)
+            for args in back_list:
+                if args[0] == h:
+                    back_copy(*args).start()
         own_back.start()
         back_r[expert] = back_s[y * NC + c]
+
+    def back_sent():
+        @pl.when(z % NC == c)
+        def _():
+            for args in back_list:
+                back_copy(*args).wait_send()
+            own_back.wait_send()
+
+    unsent.append(back_sent)
 
     eye = (iota((T, T), 0) == iota((T, T), 1)).astype(F32)
 
@@ -443,47 +533,7 @@
     lax.fori_loop(0, E, back_arrived, 0)
     o_acts[...] = mm(combine, back_r[...].reshape(MSG, 128))[:, 0:F].astype(BF)
 
-    for k in range(NY):
-        far_copy(k).wait_send()
-    for k in range(1, NY):
-        near_copy(k).wait_send()
-
-    @pl.when(c == 1)
-    def _():
-        near_copy(0).wait_send()
-
-    hub_copy().wait_send()
-    for cp in local_copies(z) + local_copies(z4):
-        cp.wait_send()
-
-    def x_sent(i, _):
-        for cp in x_copies_of(i):
-            cp.wait_send()
-        forward_right(i).wait_send()
-        return 0
-
-    lax.fori_loop(0, NZ, x_sent, 0)
-
-    def c_sent(i, _):
-        to_other_core(i // NZ, i % NZ).wait_send()
-        return 0
-
-    lax.fori_loop(0, NX * NZ, c_sent, 0)
-    for cp in sib_copies.values():
-        cp.wait_send()
-    for k in range(1, NX):
-        for q in range(NQ):
-            x_copy(k, q).wait_send()
-    for q in range(NQ):
-        @pl.when(NC * q + c != z)
-        def _():
-            z_copy(q).wait_send()
-
-    @pl.when(z % NC == c)
-    def _():
-        for args in back_list:
-            back_copy(*args).wait_send()
-        own_back.wait_send()
+    finish()
 
 
 def put(*refs):
@@ -545,10 +595,10 @@
             dma((NX * NZ,)),
             dma((NX,)),
             dma((NX,)),
-            dma((NX * NQ,)),
-            dma((NX * NQ,)),
-            dma((NQ,)),
-            dma((NZ,)),
+            dma((2 * NX * NQ,)),
+            dma((2 * NX * NQ,)),
+            dma((2 * NQ,)),
+            dma((2 * NZ,)),
             dma((E * NC,)),
             dma((E,)),
         ],

time: 70.4 us -> 67.9 us (0.964)
  Pallas kernels: 69.6 us -> 67.1 us
    pallas_call x1, Pallas kernels: 68.2 us -> 65.7 us  [body(): pl.pallas_call(kernel, name='experts_backward', out_shape=shapes, in_spec...]
where the time goes in v3:
time: 67.9 us; the launch traced here: 67.8 us
  Pallas kernels  67.1 us (99%)
    pallas_call x1, Pallas kernels, body(): pl.pallas_call(kernel, name='experts_backward', out_shape=shapes, in_spec...  65.7 us
    pallas_call x1, Pallas kernels, body(): pl.pallas_call(put, name='put', out_shape=shapes, in_specs=[pl.BlockSpec(...  1.44 us

profile of v3, /device:TPU:1, one launch (start us, length us, event | category | flops | bytes accessed | tf_op | source)
XLA Modules:
  0.0 67.8 jit_solution(9317131557338027687)
XLA Ops:
  0.6 65.7 %experts_backward.1 = (bf16[4,8,2,48,128]{4,3,2,1,0:T(8,128)(2,1)S(1)}, bf16[4,8,2,48,128]{4,3,2,1,0:T(8,128)(2,1)S(1)}, bf16[128,3072]{1,0:T(8,128)(2,1)S(1)}, bf16[48,48]{1,0:T(8,128)(2,1)S(1)}) custom-call(bf16[48,48]{1,0:T(8,128)(2,1)} %acts_h.1, bf16[48,48]{1,0:T(8,128)(2,1)} %grad_h.1, s32[2,48]{1,0:T(2,128)} %bitcast.15, f32[2,48]{1,0:T(2,128)} %bitcast.16, ...), custom_call_target="tpu_custom_call" | custom-call | tf_op jit(solution)/shard_map/experts_backward/pallas_call | solution.py:560
  66.3 1.4 %put.1 = (bf16[3072,128]{1,0:T(8,128)(2,1)}, bf16[3072,128]{1,0:T(8,128)(2,1)}, bf16[128,3072]{1,0:T(8,128)(2,1)}, bf16[48,48]{1,0:T(8,128)(2,1)}) custom-call(bf16[3072,128]{1,0:T(8,128)(2,1)S(1)} %bitcast.10, bf16[3072,128]{1,0:T(8,128)(2,1)S(1)} %bitcast.11, bf16[128,3072]{1,0:T(8,128)(2,1)S(1)} %get-tuple-element.14.refs_2_, ...), custom_call_target="tpu_custom_call" | custom-call | tf_op jit(solution)/shard_map/put/pallas_call | solution.py:623

commit v4 on v3

--- a/solution.py
+++ b/solution.py
@@ -208,7 +208,7 @@
     left, right, far = (x + NX - 1) % NX, (x + 1) % NX, (x + 2) % NX
 
     def near_z(j):
-        return z // HALF * HALF + (z + j) % HALF
+        return z // HALF * HALF + (z + j * (1 + z % HALF // 2 * 2)) % HALF
 
     def ag_copy(bx, bz, ss, to):
         blk = ag.at[bx, bz, c]
@@ -290,20 +290,22 @@
         return (near_z(j) + HALF) % NZ
 
     hub_copy().start()
+    for cp in local_copies(z):
+        cp.start()
     for cp in x_copies_of(z):
         cp.start()
-    for cp in local_copies(z):
-        cp.start()
     to_other_core(x, z).start()
-    loop(HALF, lambda j: z_arrived(near_z(j)))
+    z_arrived(near_z(1))
     x_arrived(z)
+    z_arrived(near_z(2))
+    z_arrived(near_z(3))
     ag_arrived(x, z4, c)
     for cp in local_copies(z4):
         cp.start()
     spread(z4)
     loop(HALF, lambda j: x_arrived(near_z(j)))
+    loop(HALF, lambda j: z_arrived(over(j)))
     far_arrived(z)
-    loop(HALF, lambda j: z_arrived(over(j)))
     x_arrived(z4)
     loop(HALF, lambda j: far_arrived(near_z(j)))
     loop(HALF, lambda j: x_arrived(over(j)))

time: 67.9 us -> 66.8 us (0.984)
  Pallas kernels: 67.1 us -> 66 us
    pallas_call x1, Pallas kernels: 65.7 us -> 64.6 us  [body(): pl.pallas_call(kernel, name='experts_backward', out_shape=shapes, in_spec...]
where the time goes in v4:
time: 66.8 us; the launch traced here: 66.7 us
  Pallas kernels  66 us (99%)
    pallas_call x1, Pallas kernels, body(): pl.pallas_call(kernel, name='experts_backward', out_shape=shapes, in_spec...  64.6 us
    pallas_call x1, Pallas kernels, body(): pl.pallas_call(put, name='put', out_shape=shapes, in_specs=[pl.BlockSpec(...  1.44 us

profile of v4, /device:TPU:1, one launch (start us, length us, event | category | flops | bytes accessed | tf_op | source)
XLA Modules:
  0.0 66.7 jit_solution(15743217686266054037)
XLA Ops:
  0.6 64.6 %experts_backward.1 = (bf16[4,8,2,48,128]{4,3,2,1,0:T(8,128)(2,1)S(1)}, bf16[4,8,2,48,128]{4,3,2,1,0:T(8,128)(2,1)S(1)}, bf16[128,3072]{1,0:T(8,128)(2,1)S(1)}, bf16[48,48]{1,0:T(8,128)(2,1)S(1)}) custom-call(bf16[48,48]{1,0:T(8,128)(2,1)} %acts_h.1, bf16[48,48]{1,0:T(8,128)(2,1)} %grad_h.1, s32[2,48]{1,0:T(2,128)} %bitcast.15, f32[2,48]{1,0:T(2,128)} %bitcast.16, ...), custom_call_target="tpu_custom_call" | custom-call | tf_op jit(solution)/shard_map/experts_backward/pallas_call | solution.py:562
  65.2 1.4 %put.1 = (bf16[3072,128]{1,0:T(8,128)(2,1)}, bf16[3072,128]{1,0:T(8,128)(2,1)}, bf16[128,3072]{1,0:T(8,128)(2,1)}, bf16[48,48]{1,0:T(8,128)(2,1)}) custom-call(bf16[3072,128]{1,0:T(8,128)(2,1)S(1)} %bitcast.10, bf16[3072,128]{1,0:T(8,128)(2,1)S(1)} %bitcast.11, bf16[128,3072]{1,0:T(8,128)(2,1)S(1)} %get-tuple-element.14.refs_2_, ...), custom_call_target="tpu_custom_call" | custom-call | tf_op jit(solution)/shard_map/put/pallas_call | solution.py:625
